TPU v7x, 128 devices: a whole 4x4x4 slice. The times are simulated.
128 devices in a mesh: px: 8 (over z_hi, x), py: 16 (over z_lo, y, core).
Axes of the slice: x: 4, y: 4, z: 4 (z_hi: 2, z_lo: 2; z = z_hi * 2 + z_lo), core: 2. Of those that a mesh axis runs over, the one named last changes fastest.
Arguments:
- air_state: float32 [4, 32, 128, 1024], P(None, None, 'py', 'px'), may hold values from -6 to 6
- air_bulk: float32 [32, 128, 1024], P(None, 'py', 'px'), may hold values from 0.2 to 0.5
- air_buoyancy: float32 [32], replicated, may hold values from 0.3 to 0.6
- air_wind: float32 [2, 32], replicated, may hold values from 0.05 to 0.25
- ground_state: float32 [9, 16, 1024, 128], P(None, None, ('px', 'py')), may hold values from -6 to 6
- ground_moduli: float32 [2, 16, 1024, 128], P(None, None, ('px', 'py')), may hold values from 0.05 to 0.2
- ground_buoyancy: float32 [16, 1024, 128], P(None, ('px', 'py')), may hold values from 0.3 to 0.6
Outputs:
- air_after: float32 [4, 32, 128, 1024], P(None, None, 'py', 'px')
- ground_after: float32 [9, 16, 1024, 128], P(None, None, ('px', 'py'))
All inputs are finite; a program needn't handle non-finite values.
Results may differ from a plain program's by a relative error of at most 0.00002.
Values sent between devices are 32-bit elements; how exact they have to be, the bound alone decides.
A program may use at most 128 MiB of HBM per device.

v0:
```python
import jax
import jax.numpy as jnp
from jax import lax
from jax.sharding import PartitionSpec as P

STEPS = 3


def with_halo(block, sides, width):
    for axis, dim in sides:
        count = lax.axis_size(axis)
        forward = [(i, i + 1) for i in range(count - 1)]
        backward = [(target, source) for source, target in forward]
        low = lax.ppermute(
            lax.slice_in_dim(block, block.shape[dim] - width, None, axis=dim), axis, forward
        )
        high = lax.ppermute(lax.slice_in_dim(block, 0, width, axis=dim), axis, backward)
        block = jnp.concatenate([low, block, high], axis=dim)
    return block


def padded_2(array, sides, width):
    edges = {}
    for axis, dim in sides:
        size, length = (lax.axis_size(axis), array.shape[dim])
        up = [(i, (i + 1) % size) for i in range(size - 1)]
        last = lax.slice_in_dim(array, length - width, length, axis=dim)
        leading = lax.slice_in_dim(array, 0, width, axis=dim)
        edges[dim] = (
            lax.ppermute(last, axis, up),
            lax.ppermute(leading, axis, [(b, a) for a, b in up]),
        )
    done = []
    for _, dim in sides:
        low, high = edges[dim]
        around = [(width, width) if d in done else (0, 0) for d in range(array.ndim)]
        array = jnp.concatenate([jnp.pad(low, around), array, jnp.pad(high, around)], axis=dim)
        done.append(dim)
    return array


def middle(values):
    return values[:, 1:-1, 1:-1]


def beside(values, dimension, offset):
    if dimension == 1:
        return values[:, 1 + offset : values.shape[1] - 1 + offset, 1:-1]
    return values[:, 1:-1, 1 + offset : values.shape[2] - 1 + offset]


def lower_level(values):
    return jnp.concatenate([jnp.zeros_like(values[:1]), values[:-1]], 0)


def upper_level(values):
    return jnp.concatenate([values[1:], jnp.zeros_like(values[:1])], 0)


def clear_top(stress):
    component = lax.broadcasted_iota(jnp.int32, stress.shape, 0)
    layers = lax.broadcasted_iota(jnp.int32, stress.shape, 1)
    retain = (component < 4) | (layers < stress.shape[1] - 1)
    return jnp.where(retain, stress, jnp.zeros_like(stress))


def ground_velocity(velocity, padded_stress, buoyancy, pressure_plane, x_dim, y_dim):
    stress_xx = padded_stress[0]
    stress_yy = padded_stress[1]
    stress_zz = padded_stress[2]
    stress_xy = padded_stress[3]
    stress_xz = padded_stress[4]
    stress_yz = padded_stress[5]
    middle_xy = middle(stress_xy)
    middle_xz = middle(stress_xz)
    middle_yz = middle(stress_yz)
    middle_zz = middle(stress_zz)
    force_x = (
        beside(stress_xx, x_dim, 1)
        - middle(stress_xx)
        + middle_xy
        - beside(stress_xy, y_dim, -1)
        + middle_xz
        - lower_level(middle_xz)
    )
    force_y = (
        middle_xy
        - beside(stress_xy, x_dim, -1)
        + beside(stress_yy, y_dim, 1)
        - middle(stress_yy)
        + middle_yz
        - lower_level(middle_yz)
    )
    ghost_zz = jnp.concatenate([middle_zz[1:], -pressure_plane[None]], 0)
    force_z = (
        middle_xz
        - beside(stress_xz, x_dim, -1)
        + middle_yz
        - beside(stress_yz, y_dim, -1)
        + ghost_zz
        - middle_zz
    )
    return jnp.stack(
        [
            velocity[0] + buoyancy * force_x,
            velocity[1] + buoyancy * force_y,
            velocity[2] + buoyancy * force_z,
        ]
    )


def ground_stress(stress, padded_velocity, moduli, x_dim, y_dim):
    speed_x = padded_velocity[0]
    speed_y = padded_velocity[1]
    speed_z = padded_velocity[2]
    middle_x = middle(speed_x)
    middle_y = middle(speed_y)
    middle_z = middle(speed_z)
    lambda_mod = moduli[0]
    shear_mod = moduli[1]
    longitudinal = lambda_mod + 2.0 * shear_mod
    strain_x = middle_x - beside(speed_x, x_dim, -1)
    strain_y = middle_y - beside(speed_y, y_dim, -1)
    strain_z = middle_z - lower_level(middle_z)
    stress_xx = stress[0] + longitudinal * strain_x + lambda_mod * (strain_y + strain_z)
    stress_yy = stress[1] + longitudinal * strain_y + lambda_mod * (strain_x + strain_z)
    stress_zz = stress[2] + longitudinal * strain_z + lambda_mod * (strain_x + strain_y)
    stress_xy = stress[3] + shear_mod * (
        beside(speed_x, y_dim, 1) - middle_x + beside(speed_y, x_dim, 1) - middle_y
    )
    stress_xz = stress[4] + shear_mod * (
        upper_level(middle_x) - middle_x + beside(speed_z, x_dim, 1) - middle_z
    )
    stress_yz = stress[5] + shear_mod * (
        upper_level(middle_y) - middle_y + beside(speed_z, y_dim, 1) - middle_z
    )
    stress_xz = jnp.concatenate([stress_xz[:-1], jnp.zeros_like(stress_xz[-1:])], 0)
    stress_yz = jnp.concatenate([stress_yz[:-1], jnp.zeros_like(stress_yz[-1:])], 0)
    return jnp.stack([stress_xx, stress_yy, stress_zz, stress_xy, stress_xz, stress_yz])


def window(values, row_start, row_count, col_start, col_count):
    return values[:, row_start : row_start + row_count, col_start : col_start + col_count]


def air_update(air_field, bulk, buoyancy, wind, surface, west_inner, south_inner):
    row_count = air_field.shape[2]
    col_count = air_field.shape[3]
    padded = with_halo(air_field, (("px", 3), ("py", 2)), 2)
    pressure = padded[0]
    flow_x = padded[1]
    flow_y = padded[2]
    flow_z = padded[3]
    wind_x = wind[0][:, None, None]
    wind_y = wind[1][:, None, None]
    air_buoy = buoyancy[:, None, None]
    east = window(flow_x, 2, row_count, 1, col_count + 1)
    east_next = (
        east
        - wind_x * (east - window(flow_x, 2, row_count, 0, col_count + 1))
        - wind_y * (east - window(flow_x, 1, row_count, 1, col_count + 1))
        - air_buoy
        * (
            window(pressure, 2, row_count, 2, col_count + 1)
            - window(pressure, 2, row_count, 1, col_count + 1)
        )
    )
    east_next = jnp.concatenate(
        [
            jnp.where(west_inner, east_next[:, :, :1], jnp.zeros_like(east_next[:, :, :1])),
            east_next[:, :, 1:],
        ],
        2,
    )
    north = window(flow_y, 1, row_count + 1, 2, col_count)
    north_next = (
        north
        - wind_x * (north - window(flow_y, 1, row_count + 1, 1, col_count))
        - wind_y * (north - window(flow_y, 0, row_count + 1, 2, col_count))
        - air_buoy
        * (
            window(pressure, 2, row_count + 1, 2, col_count)
            - window(pressure, 1, row_count + 1, 2, col_count)
        )
    )
    north_next = jnp.concatenate(
        [
            jnp.where(south_inner, north_next[:, :1, :], jnp.zeros_like(north_next[:, :1, :])),
            north_next[:, 1:, :],
        ],
        1,
    )
    press_mid = window(pressure, 2, row_count, 2, col_count)
    upward = window(flow_z, 2, row_count, 2, col_count)
    upward_next = (
        upward
        - wind_x * (upward - window(flow_z, 2, row_count, 1, col_count))
        - wind_y * (upward - window(flow_z, 1, row_count, 2, col_count))
        - air_buoy * (press_mid - lower_level(press_mid))
    )
    upward_next = jnp.concatenate([surface[None], upward_next[1:]], 0)
    press_next = (
        press_mid
        - wind_x * (press_mid - window(pressure, 2, row_count, 1, col_count))
        - wind_y * (press_mid - window(pressure, 1, row_count, 2, col_count))
        - bulk
        * (
            east_next[:, :, 1:]
            - east_next[:, :, :-1]
            + (north_next[:, 1:, :] - north_next[:, :-1, :])
            + (upper_level(upward_next) - upward_next)
        )
    )
    return jnp.stack([press_next, east_next[:, :, 1:], north_next[:, 1:, :], upward_next])


def strip_rim(values):
    extended = padded_2(values, ((("px", "py"), 2),), 1)
    return jnp.pad(extended, ((0, 0), (0, 0), (0, 0), (1, 1)))


def body(air_state, air_bulk, air_buoyancy, air_wind, ground_state, ground_moduli, ground_buoyancy):
    west_inner = lax.axis_index("px") > 0
    south_inner = lax.axis_index("py") > 0
    air_field = air_state
    velocity = ground_state[:3]
    stress = clear_top(ground_state[3:])
    for iteration in range(STEPS):
        pressure_plane = lax.all_to_all(
            air_field[0, 0], "py", split_axis=1, concat_axis=0, tiled=True
        ).T
        velocity = ground_velocity(
            velocity, strip_rim(stress), ground_buoyancy, pressure_plane, 1, 2
        )
        surface = lax.all_to_all(velocity[2, -1], "py", split_axis=1, concat_axis=0, tiled=True).T
        air_field = air_update(
            air_field, air_bulk, air_buoyancy, air_wind, surface, west_inner, south_inner
        )
        stress = ground_stress(stress, strip_rim(velocity), ground_moduli, 1, 2)
    ground = jnp.concatenate([velocity, stress], 0)
    return (air_field, ground)


def solution(mesh):
    placed = (
        P(None, None, "py", "px"),
        P(None, "py", "px"),
        P(),
        P(),
        P(None, None, ("px", "py"), None),
        P(None, None, ("px", "py"), None),
        P(None, ("px", "py"), None),
    )
    return jax.shard_map(
        body,
        mesh=mesh,
        in_specs=placed,
        out_specs=(P(None, None, "py", "px"), P(None, None, ("px", "py"), None)),
        check_vma=False,
    )
```

profile of v0, /device:TPU:96, one launch (start us, length us, event | category | flops | bytes accessed | tf_op | source)
XLA Modules:
  0.0 198.7 jit_solution(9225862727669534803)
XLA Ops:
  2.1 5.9 %all-to-all-start = ((f32[8,16,8]{2,0,1:T(8,128)}), f32[8,16,8]{2,0,1:T(8,128)S(1)}, u32[]{:S(2)}, u32[]{:S(2)}) async-start(f32[8,16,8]{2,0,1:T(8,128)} %copy.21), calls=%async_computation | async-start | bytes 131072 | tf_op jit(solution)/shard_map/all_to_all | solution.py:229
  8.0 1.1 slice_select_fusion
  9.2 2.0 %collective-permute-start.4 = (f32[6,16,1,128]{3,2,1,0:T(1,128)S(1)}, f32[6,16,1,128]{3,2,1,0:T(1,128)S(1)}, u32[]{:S(2)}, u32[]{:S(2)}) collective-permute-start(f32[6,16,1,128]{3,2,1,0:T(1,128)S(1)} %get-tuple-element.98), channel_id=1, source_target_pairs={{0,1},{1,2},{2,3},{3,4},{4,5},{5,6},{6,7},{7,8},{8,9},{9,10},{10,1... | collective-permute-start | bytes 147464 | tf_op jit(solution)/shard_map/ppermute | solution.py:30
  11.2 5.6 %collective-permute-start.5 = (f32[6,16,1,128]{3,2,1,0:T(1,128)S(1)}, f32[6,16,1,128]{3,2,1,0:T(1,128)S(1)}, u32[]{:S(2)}, u32[]{:S(2)}) collective-permute-start(f32[6,16,1,128]{3,2,1,0:T(1,128)S(1)} %get-tuple-element.99), channel_id=1, source_target_pairs={{1,0},{2,1},{3,2},{4,3},{5,4},{6,5},{7,6},{8,7},{9,8},{10,9},{11,1... | collective-permute-start | bytes 147464 | tf_op jit(solution)/shard_map/ppermute | solution.py:31
  16.9 2.3 %fusion.206 = (f32[4,32,8,2]{3,2,1,0:T(8,128)}, f32[4,32,8,2]{3,2,1,0:T(8,128)S(1)}) fusion(f32[4,32,8,128]{3,2,1,0:T(8,128)} %param.7), kind=kLoop, calls=%fused_computation.423 | loop fusion | bytes 32768 | tf_op jit(solution)/shard_map/slice | solution.py:15
  19.2 3.4 %collective-permute-start = (f32[4,32,8,2]{3,2,1,0:T(8,128)}, f32[4,32,8,2]{3,2,1,0:T(8,128)S(1)}, u32[]{:S(2)}, u32[]{:S(2)}) collective-permute-start(f32[4,32,8,2]{3,2,1,0:T(8,128)} %get-tuple-element.92), channel_id=1, source_target_pairs={{0,16},{16,32},{32,48},{48,64},{64,80},{80,96},{96,112},{1,17},{17... | collective-permute-start | bytes 24584 | tf_op jit(solution)/shard_map/ppermute | solution.py:14
  22.6 6.1 %collective-permute-start.1 = (f32[4,32,8,2]{3,2,1,0:T(8,128)S(1)}, f32[4,32,8,2]{3,2,1,0:T(8,128)S(1)}, u32[]{:S(2)}, u32[]{:S(2)}) collective-permute-start(f32[4,32,8,2]{3,2,1,0:T(8,128)S(1)} %get-tuple-element.93), channel_id=1, source_target_pairs={{16,0},{32,16},{48,32},{64,48},{80,64},{96,80},{112,96},{17,1},{33... | collective-permute-start | bytes 24584 | tf_op jit(solution)/shard_map/ppermute | solution.py:17
  28.7 0.9 select_maximum_fusion.4
  30.5 1.0 fusion.176
  31.5 1.1 fusion.171
  32.7 1.9 collective-permute-start.10
  34.6 5.8 %collective-permute-start.11 = (f32[3,16,1,128]{3,2,1,0:T(1,128)S(1)}, f32[3,16,1,128]{3,2,1,0:T(1,128)S(1)}, u32[]{:S(2)}, u32[]{:S(2)}) collective-permute-start(f32[3,16,1,128]{3,2,1,0:T(1,128)S(1)} %get-tuple-element.119), channel_id=1, source_target_pairs={{1,0},{2,1},{3,2},{4,3},{5,4},{6,5},{7,6},{8,7},{9,8},{10,9},{11,1... | collective-permute-start | bytes 73736 | tf_op jit(solution)/shard_map/ppermute | solution.py:31
  43.0 7.6 %all-to-all-start.1 = ((f32[8,16,8]{2,0,1:T(8,128)}), f32[8,16,8]{2,0,1:T(8,128)S(1)}, u32[]{:S(2)}, u32[]{:S(2)}) async-start(f32[8,16,8]{2,0,1:T(8,128)} %copy.23), calls=%async_computation.1 | async-start | bytes 131072 | tf_op jit(solution)/shard_map/all_to_all | solution.py:235
  51.5 0.8 bitcast_dynamic-update-slice_fusion.14
  53.0 0.8 bitcast_dynamic-update-slice_fusion.12
  53.8 0.8 bitcast_dynamic-update-slice_fusion.11
  54.9 2.0 %collective-permute-start.12 = (f32[6,16,1,128]{3,2,1,0:T(1,128)S(1)}, f32[6,16,1,128]{3,2,1,0:T(1,128)S(1)}, u32[]{:S(2)}, u32[]{:S(2)}) collective-permute-start(f32[6,16,1,128]{3,2,1,0:T(1,128)S(1)} %get-tuple-element.96), channel_id=1, source_target_pairs={{0,1},{1,2},{2,3},{3,4},{4,5},{5,6},{6,7},{7,8},{8,9},{9,10},{10,1... | collective-permute-start | bytes 147464 | tf_op jit(solution)/shard_map/ppermute | solution.py:30
  56.9 5.6 %collective-permute-start.13 = (f32[6,16,1,128]{3,2,1,0:T(1,128)S(1)}, f32[6,16,1,128]{3,2,1,0:T(1,128)S(1)}, u32[]{:S(2)}, u32[]{:S(2)}) collective-permute-start(f32[6,16,1,128]{3,2,1,0:T(1,128)S(1)} %get-tuple-element.97), channel_id=1, source_target_pairs={{1,0},{2,1},{3,2},{4,3},{5,4},{6,5},{7,6},{8,7},{9,8},{10,9},{11,1... | collective-permute-start | bytes 147464 | tf_op jit(solution)/shard_map/ppermute | solution.py:31
  62.6 1.7 pad_maximum_fusion.20
  64.3 1.9 collective-permute-start.2
  66.2 5.8 %collective-permute-start.3 = (f32[4,32,2,132]{3,2,1,0:T(2,128)}, f32[4,32,2,132]{3,2,1,0:T(2,128)}, u32[]{:S(2)}, u32[]{:S(2)}) collective-permute-start(f32[4,32,2,132]{3,2,1,0:T(2,128)} %get-tuple-element.67), channel_id=1, source_target_pairs={{1,0},{2,1},{3,2},{4,3},{5,4},{6,5},{7,6},{8,7},{9,8},{10,9},{11,1... | collective-permute-start | bytes 405512 | tf_op jit(solution)/shard_map/ppermute | solution.py:17
  72.7 0.9 select_maximum_fusion.2
  74.9 1.3 collective-permute-done.3
  76.2 2.0 %pad_maximum_fusion = f32[4,32,12,132]{3,2,1,0:T(8,128)S(1)} fusion(f32[4,32,2,132]{3,2,1,0:T(2,128)} %collective-permute-done.3, f32[4,32,8,2]{3,2,1,0:T(8,128)S(1)} %collective-permute-done.1, f32[4,32,8,128]{3,2,1,0:T(8,128)S(1)} %copy-done.1, f32[4,32,8,2]{3,2,1,0:T(8,128)S(1)} %collective-permute-done, f32[4,32,2,132]{3,2,1,0:T(2,128)} %collective-permute-done.2), kind=kLoop, calls=%fused_computation.2 | loop fusion | flops 811008 | bytes 1622016 | tf_op jit(solution)/shard_map/concatenate | solution.py:18
  81.2 5.9 %all-to-all-start.2 = ((f32[8,16,8]{2,0,1:T(8,128)}), f32[8,16,8]{2,0,1:T(8,128)S(1)}, u32[]{:S(2)}, u32[]{:S(2)}) async-start(f32[8,16,8]{2,0,1:T(8,128)} %copy.25), calls=%async_computation.2 | async-start | bytes 131072 | tf_op jit(solution)/shard_map/all_to_all | solution.py:229
  87.1 4.8 %all-to-all-done.2 = f32[8,16,8]{2,0,1:T(8,128)S(1)} async-done(((f32[8,16,8]{2,0,1:T(8,128)}), f32[8,16,8]{2,0,1:T(8,128)S(1)}, u32[]{:S(2)}, u32[]{:S(2)}) %all-to-all-start.2) | async-done | bytes 4128 | tf_op jit(solution)/shard_map/all_to_all | solution.py:229
  92.9 4.7 %all-to-all-start.3 = ((f32[8,16,8]{2,0,1:T(8,128)}), f32[8,16,8]{2,0,1:T(8,128)S(1)}, u32[]{:S(2)}, u32[]{:S(2)}) async-start(f32[8,16,8]{2,0,1:T(8,128)} %copy.27), calls=%async_computation.3 | async-start | bytes 131072 | tf_op jit(solution)/shard_map/all_to_all | solution.py:235
  97.7 2.0 %collective-permute-start.18 = (f32[3,16,1,128]{3,2,1,0:T(1,128)S(1)}, f32[3,16,1,128]{3,2,1,0:T(1,128)S(1)}, u32[]{:S(2)}, u32[]{:S(2)}) collective-permute-start(f32[3,16,1,128]{3,2,1,0:T(1,128)S(1)} %get-tuple-element.116), channel_id=1, source_target_pairs={{0,1},{1,2},{2,3},{3,4},{4,5},{5,6},{6,7},{7,8},{8,9},{9,10},{10,1... | collective-permute-start | bytes 73736 | tf_op jit(solution)/shard_map/ppermute | solution.py:30
  99.7 5.6 %collective-permute-start.19 = (f32[3,16,1,128]{3,2,1,0:T(1,128)S(1)}, f32[3,16,1,128]{3,2,1,0:T(1,128)S(1)}, u32[]{:S(2)}, u32[]{:S(2)}) collective-permute-start(f32[3,16,1,128]{3,2,1,0:T(1,128)S(1)} %get-tuple-element.117), channel_id=1, source_target_pairs={{1,0},{2,1},{3,2},{4,3},{5,4},{6,5},{7,6},{8,7},{9,8},{10,9},{11,1... | collective-permute-start | bytes 73736 | tf_op jit(solution)/shard_map/ppermute | solution.py:31
  105.4 1.0 fusion.204
  106.4 1.9 collective-permute-start.6
  108.3 7.7 %collective-permute-start.7 = (f32[4,32,8,2]{3,2,1,0:T(8,128)S(1)}, f32[4,32,8,2]{3,2,1,0:T(8,128)S(1)}, u32[]{:S(2)}, u32[]{:S(2)}) collective-permute-start(f32[4,32,8,2]{3,2,1,0:T(8,128)S(1)} %get-tuple-element.88), channel_id=1, source_target_pairs={{16,0},{32,16},{48,32},{64,48},{80,64},{96,80},{112,96},{17,1},{33... | collective-permute-start | bytes 24584 | tf_op jit(solution)/shard_map/ppermute | solution.py:17
  117.5 1.6 bitcast_dynamic-update-slice_fusion.8
  119.1 1.6 bitcast_dynamic-update-slice_fusion.7
  120.7 0.8 bitcast_dynamic-update-slice_fusion.6
  121.5 0.8 bitcast_dynamic-update-slice_fusion.5
  123.2 1.9 collective-permute-start.20
  125.1 5.8 %collective-permute-start.21 = (f32[6,16,1,128]{3,2,1,0:T(1,128)S(1)}, f32[6,16,1,128]{3,2,1,0:T(1,128)S(1)}, u32[]{:S(2)}, u32[]{:S(2)}) collective-permute-start(f32[6,16,1,128]{3,2,1,0:T(1,128)S(1)} %get-tuple-element.95), channel_id=1, source_target_pairs={{1,0},{2,1},{3,2},{4,3},{5,4},{6,5},{7,6},{8,7},{9,8},{10,9},{11,1... | collective-permute-start | bytes 147464 | tf_op jit(solution)/shard_map/ppermute | solution.py:31
  130.9 0.9 pad_maximum_fusion.17
  131.8 1.9 collective-permute-start.8
  133.7 5.8 %collective-permute-start.9 = (f32[4,32,2,132]{3,2,1,0:T(2,128)S(1)}, f32[4,32,2,132]{3,2,1,0:T(2,128)S(1)}, u32[]{:S(2)}, u32[]{:S(2)}) collective-permute-start(f32[4,32,2,132]{3,2,1,0:T(2,128)S(1)} %get-tuple-element.65), channel_id=1, source_target_pairs={{1,0},{2,1},{3,2},{4,3},{5,4},{6,5},{7,6},{8,7},{9,8},{10,9},{11,1... | collective-permute-start | bytes 405512 | tf_op jit(solution)/shard_map/ppermute | solution.py:17
  139.5 0.9 select_maximum_fusion
  141.5 0.8 constant_dynamic-update-slice_fusion.2
  142.3 0.8 constant_dynamic-update-slice_fusion.1
  143.3 1.0 pad_maximum_fusion.1
  147.4 5.9 %all-to-all-start.4 = ((f32[8,16,8]{2,0,1:T(8,128)}), f32[8,16,8]{2,0,1:T(8,128)S(1)}, u32[]{:S(2)}, u32[]{:S(2)}) async-start(f32[8,16,8]{2,0,1:T(8,128)} %copy.29), calls=%async_computation.4 | async-start | bytes 131072 | tf_op jit(solution)/shard_map/all_to_all | solution.py:229
  153.3 1.1 fusion.202
  154.4 1.9 collective-permute-start.14
  156.3 7.5 %collective-permute-start.15 = (f32[4,32,8,2]{3,2,1,0:T(8,128)}, f32[4,32,8,2]{3,2,1,0:T(8,128)S(1)}, u32[]{:S(2)}, u32[]{:S(2)}) collective-permute-start(f32[4,32,8,2]{3,2,1,0:T(8,128)} %get-tuple-element.83), channel_id=1, source_target_pairs={{16,0},{32,16},{48,32},{64,48},{80,64},{96,80},{112,96},{17,1},{33... | collective-permute-start | bytes 24584 | tf_op jit(solution)/shard_map/ppermute | solution.py:17
  164.0 1.7 constant_dynamic-update-slice_fusion
  166.4 5.7 %all-to-all-start.5 = ((f32[8,16,8]{2,0,1:T(8,128)}), f32[8,16,8]{2,0,1:T(8,128)S(1)}, u32[]{:S(2)}, u32[]{:S(2)}) async-start(f32[8,16,8]{2,0,1:T(8,128)} %copy.31), calls=%async_computation.5 | async-start | bytes 131072 | tf_op jit(solution)/shard_map/all_to_all | solution.py:235
  172.2 2.0 %collective-permute-start.22 = (f32[3,16,1,128]{3,2,1,0:T(1,128)S(1)}, f32[3,16,1,128]{3,2,1,0:T(1,128)S(1)}, u32[]{:S(2)}, u32[]{:S(2)}) collective-permute-start(f32[3,16,1,128]{3,2,1,0:T(1,128)S(1)} %get-tuple-element.114), channel_id=1, source_target_pairs={{0,1},{1,2},{2,3},{3,4},{4,5},{5,6},{6,7},{7,8},{8,9},{9,10},{10,1... | collective-permute-start | bytes 73736 | tf_op jit(solution)/shard_map/ppermute | solution.py:30
  174.2 5.6 %collective-permute-start.23 = (f32[3,16,1,128]{3,2,1,0:T(1,128)S(1)}, f32[3,16,1,128]{3,2,1,0:T(1,128)S(1)}, u32[]{:S(2)}, u32[]{:S(2)}) collective-permute-start(f32[3,16,1,128]{3,2,1,0:T(1,128)S(1)} %get-tuple-element.115), channel_id=1, source_target_pairs={{1,0},{2,1},{3,2},{4,3},{5,4},{6,5},{7,6},{8,7},{9,8},{10,9},{11,1... | collective-permute-start | bytes 73736 | tf_op jit(solution)/shard_map/ppermute | solution.py:31
  180.0 0.9 pad_maximum_fusion.11
  180.9 2.1 %collective-permute-start.16 = (f32[4,32,2,132]{3,2,1,0:T(2,128)S(1)}, f32[4,32,2,132]{3,2,1,0:T(2,128)S(1)}, u32[]{:S(2)}, u32[]{:S(2)}) collective-permute-start(f32[4,32,2,132]{3,2,1,0:T(2,128)S(1)} %get-tuple-element.56), channel_id=1, source_target_pairs={{0,1},{1,2},{2,3},{3,4},{4,5},{5,6},{6,7},{7,8},{8,9},{9,10},{10,1... | collective-permute-start | bytes 405512 | tf_op jit(solution)/shard_map/ppermute | solution.py:14
  182.9 6.1 %collective-permute-start.17 = (f32[4,32,2,132]{3,2,1,0:T(2,128)S(1)}, f32[4,32,2,132]{3,2,1,0:T(2,128)S(1)}, u32[]{:S(2)}, u32[]{:S(2)}) collective-permute-start(f32[4,32,2,132]{3,2,1,0:T(2,128)S(1)} %get-tuple-element.57), channel_id=1, source_target_pairs={{1,0},{2,1},{3,2},{4,3},{5,4},{6,5},{7,6},{8,7},{9,8},{10,9},{11,1... | collective-permute-start | bytes 405512 | tf_op jit(solution)/shard_map/ppermute | solution.py:17
  189.9 0.8 bitcast_dynamic-update-slice_fusion.2
  190.7 0.8 bitcast_dynamic-update-slice_fusion.1
  191.5 0.8 bitcast_dynamic-update-slice_fusion
  192.2 0.8 fusion.108
  193.0 0.8 fusion.103
  193.8 0.8 fusion.97
  194.6 1.0 pad_maximum_fusion.2
  197.8 0.8 pad_maximum_fusion.5
  (194 shorter events, 23.2 us)
Async XLA Ops:
  2.1 26.6 %all-to-all-start = ((f32[8,16,8]{2,0,1:T(8,128)}), f32[8,16,8]{2,0,1:T(8,128)S(1)}, u32[]{:S(2)}, u32[]{:S(2)}) async-start(f32[8,16,8]{2,0,1:T(8,128)} %copy.21), calls=%async_computation | async-start | bytes 131072 | tf_op jit(solution)/shard_map/all_to_all | solution.py:229
  9.2 19.5 %collective-permute-start.4 = (f32[6,16,1,128]{3,2,1,0:T(1,128)S(1)}, f32[6,16,1,128]{3,2,1,0:T(1,128)S(1)}, u32[]{:S(2)}, u32[]{:S(2)}) collective-permute-start(f32[6,16,1,128]{3,2,1,0:T(1,128)S(1)} %get-tuple-element.98), channel_id=1, source_target_pairs={{0,1},{1,2},{2,3},{3,4},{4,5},{5,6},{6,7},{7,8},{8,9},{9,10},{10,1... | collective-permute-start | bytes 147464 | tf_op jit(solution)/shard_map/ppermute | solution.py:30
  11.2 17.5 %collective-permute-start.5 = (f32[6,16,1,128]{3,2,1,0:T(1,128)S(1)}, f32[6,16,1,128]{3,2,1,0:T(1,128)S(1)}, u32[]{:S(2)}, u32[]{:S(2)}) collective-permute-start(f32[6,16,1,128]{3,2,1,0:T(1,128)S(1)} %get-tuple-element.99), channel_id=1, source_target_pairs={{1,0},{2,1},{3,2},{4,3},{5,4},{6,5},{7,6},{8,7},{9,8},{10,9},{11,1... | collective-permute-start | bytes 147464 | tf_op jit(solution)/shard_map/ppermute | solution.py:31
  19.2 43.4 %collective-permute-start = (f32[4,32,8,2]{3,2,1,0:T(8,128)}, f32[4,32,8,2]{3,2,1,0:T(8,128)S(1)}, u32[]{:S(2)}, u32[]{:S(2)}) collective-permute-start(f32[4,32,8,2]{3,2,1,0:T(8,128)} %get-tuple-element.92), channel_id=1, source_target_pairs={{0,16},{16,32},{32,48},{48,64},{64,80},{80,96},{96,112},{1,17},{17... | collective-permute-start | bytes 24584 | tf_op jit(solution)/shard_map/ppermute | solution.py:14
  22.6 40.0 %collective-permute-start.1 = (f32[4,32,8,2]{3,2,1,0:T(8,128)S(1)}, f32[4,32,8,2]{3,2,1,0:T(8,128)S(1)}, u32[]{:S(2)}, u32[]{:S(2)}) collective-permute-start(f32[4,32,8,2]{3,2,1,0:T(8,128)S(1)} %get-tuple-element.93), channel_id=1, source_target_pairs={{16,0},{32,16},{48,32},{64,48},{80,64},{96,80},{112,96},{17,1},{33... | collective-permute-start | bytes 24584 | tf_op jit(solution)/shard_map/ppermute | solution.py:17
  29.7 0.8 copy-start.2
  29.7 10.7 %copy-start.27 = (f32[2,32]{1,0:T(2,128)S(1)}, f32[2,32]{1,0:T(2,128)}, u32[]{:S(2)}) copy-start(f32[2,32]{1,0:T(2,128)} %param.10) | copy-start | bytes 772
  29.7 10.7 %copy-start.14 = (f32[32]{0:T(128)S(1)}, f32[32]{0:T(128)}, u32[]{:S(2)}) copy-start(f32[32]{0:T(128)} %param.9) | copy-start | bytes 388
  31.5 20.0 %copy-start = (f32[2,16,8,128]{3,2,1,0:T(8,128)S(1)}, f32[2,16,8,128]{3,2,1,0:T(8,128)}, u32[]{:S(2)}) copy-start(f32[2,16,8,128]{3,2,1,0:T(8,128)} %param.12) | copy-start | bytes 393220
  32.7 18.0 %collective-permute-start.10 = (f32[3,16,1,128]{3,2,1,0:T(1,128)S(1)}, f32[3,16,1,128]{3,2,1,0:T(1,128)S(1)}, u32[]{:S(2)}, u32[]{:S(2)}) collective-permute-start(f32[3,16,1,128]{3,2,1,0:T(1,128)S(1)} %get-tuple-element.118), channel_id=1, source_target_pairs={{0,1},{1,2},{2,3},{3,4},{4,5},{5,6},{6,7},{7,8},{8,9},{9,10},{10,1... | collective-permute-start | bytes 73736 | tf_op jit(solution)/shard_map/ppermute | solution.py:30
  34.6 16.1 %collective-permute-start.11 = (f32[3,16,1,128]{3,2,1,0:T(1,128)S(1)}, f32[3,16,1,128]{3,2,1,0:T(1,128)S(1)}, u32[]{:S(2)}, u32[]{:S(2)}) collective-permute-start(f32[3,16,1,128]{3,2,1,0:T(1,128)S(1)} %get-tuple-element.119), channel_id=1, source_target_pairs={{1,0},{2,1},{3,2},{4,3},{5,4},{6,5},{7,6},{8,7},{9,8},{10,9},{11,1... | collective-permute-start | bytes 73736 | tf_op jit(solution)/shard_map/ppermute | solution.py:31
  43.0 29.0 %all-to-all-start.1 = ((f32[8,16,8]{2,0,1:T(8,128)}), f32[8,16,8]{2,0,1:T(8,128)S(1)}, u32[]{:S(2)}, u32[]{:S(2)}) async-start(f32[8,16,8]{2,0,1:T(8,128)} %copy.23), calls=%async_computation.1 | async-start | bytes 131072 | tf_op jit(solution)/shard_map/all_to_all | solution.py:235
  51.1 3.4 %copy-start.15 = (pred[16]{0:T(512)(128)(4,1)S(1)}, pred[16]{0:T(512)(128)(4,1)}, u32[]{:S(2)}) copy-start(pred[16]{0:T(512)(128)(4,1)} %constant.29.clone.1) | copy-start | bytes 52
  51.3 11.3 %copy-start.1 = (f32[4,32,8,128]{3,2,1,0:T(8,128)S(1)}, f32[4,32,8,128]{3,2,1,0:T(8,128)}, u32[]{:S(2)}) copy-start(f32[4,32,8,128]{3,2,1,0:T(8,128)} %param.7) | copy-start | bytes 1572868
  54.9 17.7 %collective-permute-start.12 = (f32[6,16,1,128]{3,2,1,0:T(1,128)S(1)}, f32[6,16,1,128]{3,2,1,0:T(1,128)S(1)}, u32[]{:S(2)}, u32[]{:S(2)}) collective-permute-start(f32[6,16,1,128]{3,2,1,0:T(1,128)S(1)} %get-tuple-element.96), channel_id=1, source_target_pairs={{0,1},{1,2},{2,3},{3,4},{4,5},{5,6},{6,7},{7,8},{8,9},{9,10},{10,1... | collective-permute-start | bytes 147464 | tf_op jit(solution)/shard_map/ppermute | solution.py:30
  56.9 15.7 %collective-permute-start.13 = (f32[6,16,1,128]{3,2,1,0:T(1,128)S(1)}, f32[6,16,1,128]{3,2,1,0:T(1,128)S(1)}, u32[]{:S(2)}, u32[]{:S(2)}) collective-permute-start(f32[6,16,1,128]{3,2,1,0:T(1,128)S(1)} %get-tuple-element.97), channel_id=1, source_target_pairs={{1,0},{2,1},{3,2},{4,3},{5,4},{6,5},{7,6},{8,7},{9,8},{10,9},{11,1... | collective-permute-start | bytes 147464 | tf_op jit(solution)/shard_map/ppermute | solution.py:31
  64.3 10.6 %collective-permute-start.2 = (f32[4,32,2,132]{3,2,1,0:T(2,128)}, f32[4,32,2,132]{3,2,1,0:T(2,128)}, u32[]{:S(2)}, u32[]{:S(2)}) collective-permute-start(f32[4,32,2,132]{3,2,1,0:T(2,128)} %get-tuple-element.66), channel_id=1, source_target_pairs={{0,1},{1,2},{2,3},{3,4},{4,5},{5,6},{6,7},{7,8},{8,9},{9,10},{10,1... | collective-permute-start | bytes 405512 | tf_op jit(solution)/shard_map/ppermute | solution.py:14
  66.2 9.9 %collective-permute-start.3 = (f32[4,32,2,132]{3,2,1,0:T(2,128)}, f32[4,32,2,132]{3,2,1,0:T(2,128)}, u32[]{:S(2)}, u32[]{:S(2)}) collective-permute-start(f32[4,32,2,132]{3,2,1,0:T(2,128)} %get-tuple-element.67), channel_id=1, source_target_pairs={{1,0},{2,1},{3,2},{4,3},{5,4},{6,5},{7,6},{8,7},{9,8},{10,9},{11,1... | collective-permute-start | bytes 405512 | tf_op jit(solution)/shard_map/ppermute | solution.py:17
  79.0 0.9 copy-start.18
  79.1 0.9 copy-start.21
  79.1 0.9 copy-start.24
  79.1 1.1 copy-start.3
  79.1 1.1 copy-start.17
  79.8 12.2 %copy-start.13 = (f32[15,8,128]{2,1,0:T(8,128)S(1)}, f32[15,8,128]{2,1,0:T(8,128)}, u32[]{:S(2)}) copy-start(f32[15,8,128]{2,1,0:T(8,128)} %slice.1109) | copy-start | bytes 184324
  81.2 10.7 %all-to-all-start.2 = ((f32[8,16,8]{2,0,1:T(8,128)}), f32[8,16,8]{2,0,1:T(8,128)S(1)}, u32[]{:S(2)}, u32[]{:S(2)}) async-start(f32[8,16,8]{2,0,1:T(8,128)} %copy.25), calls=%async_computation.2 | async-start | bytes 131072 | tf_op jit(solution)/shard_map/all_to_all | solution.py:229
  92.9 23.1 %all-to-all-start.3 = ((f32[8,16,8]{2,0,1:T(8,128)}), f32[8,16,8]{2,0,1:T(8,128)S(1)}, u32[]{:S(2)}, u32[]{:S(2)}) async-start(f32[8,16,8]{2,0,1:T(8,128)} %copy.27), calls=%async_computation.3 | async-start | bytes 131072 | tf_op jit(solution)/shard_map/all_to_all | solution.py:235
  97.7 19.0 %collective-permute-start.18 = (f32[3,16,1,128]{3,2,1,0:T(1,128)S(1)}, f32[3,16,1,128]{3,2,1,0:T(1,128)S(1)}, u32[]{:S(2)}, u32[]{:S(2)}) collective-permute-start(f32[3,16,1,128]{3,2,1,0:T(1,128)S(1)} %get-tuple-element.116), channel_id=1, source_target_pairs={{0,1},{1,2},{2,3},{3,4},{4,5},{5,6},{6,7},{7,8},{8,9},{9,10},{10,1... | collective-permute-start | bytes 73736 | tf_op jit(solution)/shard_map/ppermute | solution.py:30
  99.7 17.0 %collective-permute-start.19 = (f32[3,16,1,128]{3,2,1,0:T(1,128)S(1)}, f32[3,16,1,128]{3,2,1,0:T(1,128)S(1)}, u32[]{:S(2)}, u32[]{:S(2)}) collective-permute-start(f32[3,16,1,128]{3,2,1,0:T(1,128)S(1)} %get-tuple-element.117), channel_id=1, source_target_pairs={{1,0},{2,1},{3,2},{4,3},{5,4},{6,5},{7,6},{8,7},{9,8},{10,9},{11,1... | collective-permute-start | bytes 73736 | tf_op jit(solution)/shard_map/ppermute | solution.py:31
  106.4 24.5 %collective-permute-start.6 = (f32[4,32,8,2]{3,2,1,0:T(8,128)}, f32[4,32,8,2]{3,2,1,0:T(8,128)S(1)}, u32[]{:S(2)}, u32[]{:S(2)}) collective-permute-start(f32[4,32,8,2]{3,2,1,0:T(8,128)} %get-tuple-element.87), channel_id=1, source_target_pairs={{0,16},{16,32},{32,48},{48,64},{64,80},{80,96},{96,112},{1,17},{17... | collective-permute-start | bytes 24584 | tf_op jit(solution)/shard_map/ppermute | solution.py:14
  108.3 22.6 %collective-permute-start.7 = (f32[4,32,8,2]{3,2,1,0:T(8,128)S(1)}, f32[4,32,8,2]{3,2,1,0:T(8,128)S(1)}, u32[]{:S(2)}, u32[]{:S(2)}) collective-permute-start(f32[4,32,8,2]{3,2,1,0:T(8,128)S(1)} %get-tuple-element.88), channel_id=1, source_target_pairs={{16,0},{32,16},{48,32},{64,48},{80,64},{96,80},{112,96},{17,1},{33... | collective-permute-start | bytes 24584 | tf_op jit(solution)/shard_map/ppermute | solution.py:17
  116.7 4.0 %copy-start.11 = (f32[16,8,128]{2,1,0:T(8,128)S(1)}, f32[16,8,128]{2,1,0:T(8,128)}, u32[]{:S(2)}) copy-start(f32[16,8,128]{2,1,0:T(8,128)} %get-tuple-element.27) | copy-start | bytes 196612
  117.2 4.3 %copy-start.10 = (f32[16,8,128]{2,1,0:T(8,128)S(1)}, f32[16,8,128]{2,1,0:T(8,128)}, u32[]{:S(2)}) copy-start(f32[16,8,128]{2,1,0:T(8,128)} %get-tuple-element.25) | copy-start | bytes 196612
  123.2 16.3 %collective-permute-start.20 = (f32[6,16,1,128]{3,2,1,0:T(1,128)S(1)}, f32[6,16,1,128]{3,2,1,0:T(1,128)S(1)}, u32[]{:S(2)}, u32[]{:S(2)}) collective-permute-start(f32[6,16,1,128]{3,2,1,0:T(1,128)S(1)} %get-tuple-element.94), channel_id=1, source_target_pairs={{0,1},{1,2},{2,3},{3,4},{4,5},{5,6},{6,7},{7,8},{8,9},{9,10},{10,1... | collective-permute-start | bytes 147464 | tf_op jit(solution)/shard_map/ppermute | solution.py:30
  125.1 14.4 %collective-permute-start.21 = (f32[6,16,1,128]{3,2,1,0:T(1,128)S(1)}, f32[6,16,1,128]{3,2,1,0:T(1,128)S(1)}, u32[]{:S(2)}, u32[]{:S(2)}) collective-permute-start(f32[6,16,1,128]{3,2,1,0:T(1,128)S(1)} %get-tuple-element.95), channel_id=1, source_target_pairs={{1,0},{2,1},{3,2},{4,3},{5,4},{6,5},{7,6},{8,7},{9,8},{10,9},{11,1... | collective-permute-start | bytes 147464 | tf_op jit(solution)/shard_map/ppermute | solution.py:31
  131.8 11.3 %collective-permute-start.8 = (f32[4,32,2,132]{3,2,1,0:T(2,128)S(1)}, f32[4,32,2,132]{3,2,1,0:T(2,128)S(1)}, u32[]{:S(2)}, u32[]{:S(2)}) collective-permute-start(f32[4,32,2,132]{3,2,1,0:T(2,128)S(1)} %get-tuple-element.64), channel_id=1, source_target_pairs={{0,1},{1,2},{2,3},{3,4},{4,5},{5,6},{6,7},{7,8},{8,9},{9,10},{10,1... | collective-permute-start | bytes 405512 | tf_op jit(solution)/shard_map/ppermute | solution.py:14
  133.7 9.6 %collective-permute-start.9 = (f32[4,32,2,132]{3,2,1,0:T(2,128)S(1)}, f32[4,32,2,132]{3,2,1,0:T(2,128)S(1)}, u32[]{:S(2)}, u32[]{:S(2)}) collective-permute-start(f32[4,32,2,132]{3,2,1,0:T(2,128)S(1)} %get-tuple-element.65), channel_id=1, source_target_pairs={{1,0},{2,1},{3,2},{4,3},{5,4},{6,5},{7,6},{8,7},{9,8},{10,9},{11,1... | collective-permute-start | bytes 405512 | tf_op jit(solution)/shard_map/ppermute | solution.py:17
  140.6 2.5 %copy-start.4 = (f32[16,10,130]{2,1,0:T(8,128)}, f32[16,10,130]{2,1,0:T(8,128)S(1)}, u32[]{:S(2)}) copy-start(f32[16,10,130]{2,1,0:T(8,128)S(1)} %get-tuple-element.44) | copy-start | bytes 249604
  145.1 1.0 copy-start.19
  145.1 1.0 copy-start.22
  145.1 1.0 copy-start.25
  145.2 1.2 copy-start.16
  146.7 17.3 %copy-start.12 = (f32[15,8,128]{2,1,0:T(8,128)S(1)}, f32[15,8,128]{2,1,0:T(8,128)}, u32[]{:S(2)}) copy-start(f32[15,8,128]{2,1,0:T(8,128)} %slice.1183) | copy-start | bytes 184324
  147.4 16.5 %all-to-all-start.4 = ((f32[8,16,8]{2,0,1:T(8,128)}), f32[8,16,8]{2,0,1:T(8,128)S(1)}, u32[]{:S(2)}, u32[]{:S(2)}) async-start(f32[8,16,8]{2,0,1:T(8,128)} %copy.29), calls=%async_computation.4 | async-start | bytes 131072 | tf_op jit(solution)/shard_map/all_to_all | solution.py:229
  154.4 25.5 %collective-permute-start.14 = (f32[4,32,8,2]{3,2,1,0:T(8,128)}, f32[4,32,8,2]{3,2,1,0:T(8,128)S(1)}, u32[]{:S(2)}, u32[]{:S(2)}) collective-permute-start(f32[4,32,8,2]{3,2,1,0:T(8,128)} %get-tuple-element.82), channel_id=1, source_target_pairs={{0,16},{16,32},{32,48},{48,64},{64,80},{80,96},{96,112},{1,17},{17... | collective-permute-start | bytes 24584 | tf_op jit(solution)/shard_map/ppermute | solution.py:14
  156.3 23.6 %collective-permute-start.15 = (f32[4,32,8,2]{3,2,1,0:T(8,128)}, f32[4,32,8,2]{3,2,1,0:T(8,128)S(1)}, u32[]{:S(2)}, u32[]{:S(2)}) collective-permute-start(f32[4,32,8,2]{3,2,1,0:T(8,128)} %get-tuple-element.83), channel_id=1, source_target_pairs={{16,0},{32,16},{48,32},{64,48},{80,64},{96,80},{112,96},{17,1},{33... | collective-permute-start | bytes 24584 | tf_op jit(solution)/shard_map/ppermute | solution.py:17
  166.4 13.4 %all-to-all-start.5 = ((f32[8,16,8]{2,0,1:T(8,128)}), f32[8,16,8]{2,0,1:T(8,128)S(1)}, u32[]{:S(2)}, u32[]{:S(2)}) async-start(f32[8,16,8]{2,0,1:T(8,128)} %copy.31), calls=%async_computation.5 | async-start | bytes 131072 | tf_op jit(solution)/shard_map/all_to_all | solution.py:235
  172.2 16.9 %collective-permute-start.22 = (f32[3,16,1,128]{3,2,1,0:T(1,128)S(1)}, f32[3,16,1,128]{3,2,1,0:T(1,128)S(1)}, u32[]{:S(2)}, u32[]{:S(2)}) collective-permute-start(f32[3,16,1,128]{3,2,1,0:T(1,128)S(1)} %get-tuple-element.114), channel_id=1, source_target_pairs={{0,1},{1,2},{2,3},{3,4},{4,5},{5,6},{6,7},{7,8},{8,9},{9,10},{10,1... | collective-permute-start | bytes 73736 | tf_op jit(solution)/shard_map/ppermute | solution.py:30
  174.2 14.8 %collective-permute-start.23 = (f32[3,16,1,128]{3,2,1,0:T(1,128)S(1)}, f32[3,16,1,128]{3,2,1,0:T(1,128)S(1)}, u32[]{:S(2)}, u32[]{:S(2)}) collective-permute-start(f32[3,16,1,128]{3,2,1,0:T(1,128)S(1)} %get-tuple-element.115), channel_id=1, source_target_pairs={{1,0},{2,1},{3,2},{4,3},{5,4},{6,5},{7,6},{8,7},{9,8},{10,9},{11,1... | collective-permute-start | bytes 73736 | tf_op jit(solution)/shard_map/ppermute | solution.py:31
  180.0 10.0 %copy-start.6 = (f32[16,8,128]{2,1,0:T(8,128)S(1)}, f32[16,8,128]{2,1,0:T(8,128)}, u32[]{:S(2)}) copy-start(f32[16,8,128]{2,1,0:T(8,128)} %get-tuple-element.19) | copy-start | bytes 196612
  180.9 9.8 %copy-start.7 = (f32[16,8,128]{2,1,0:T(8,128)S(1)}, f32[16,8,128]{2,1,0:T(8,128)}, u32[]{:S(2)}) copy-start(f32[16,8,128]{2,1,0:T(8,128)} %get-tuple-element.17) | copy-start | bytes 196612
  180.9 13.7 %collective-permute-start.16 = (f32[4,32,2,132]{3,2,1,0:T(2,128)S(1)}, f32[4,32,2,132]{3,2,1,0:T(2,128)S(1)}, u32[]{:S(2)}, u32[]{:S(2)}) collective-permute-start(f32[4,32,2,132]{3,2,1,0:T(2,128)S(1)} %get-tuple-element.56), channel_id=1, source_target_pairs={{0,1},{1,2},{2,3},{3,4},{4,5},{5,6},{6,7},{7,8},{8,9},{9,10},{10,1... | collective-permute-start | bytes 405512 | tf_op jit(solution)/shard_map/ppermute | solution.py:14
  182.9 8.5 %copy-start.8 = (f32[16,8,128]{2,1,0:T(8,128)S(1)}, f32[16,8,128]{2,1,0:T(8,128)}, u32[]{:S(2)}) copy-start(f32[16,8,128]{2,1,0:T(8,128)} %get-tuple-element.15) | copy-start | bytes 196612
  182.9 11.6 %collective-permute-start.17 = (f32[4,32,2,132]{3,2,1,0:T(2,128)S(1)}, f32[4,32,2,132]{3,2,1,0:T(2,128)S(1)}, u32[]{:S(2)}, u32[]{:S(2)}) collective-permute-start(f32[4,32,2,132]{3,2,1,0:T(2,128)S(1)} %get-tuple-element.57), channel_id=1, source_target_pairs={{1,0},{2,1},{3,2},{4,3},{5,4},{6,5},{7,6},{8,7},{9,8},{10,9},{11,1... | collective-permute-start | bytes 405512 | tf_op jit(solution)/shard_map/ppermute | solution.py:17
  189.6 2.7 %copy-start.9 = (f32[16,8,128]{2,1,0:T(8,128)S(1)}, f32[16,8,128]{2,1,0:T(8,128)}, u32[]{:S(2)}) copy-start(f32[16,8,128]{2,1,0:T(8,128)} %get-tuple-element.13) | copy-start | bytes 196612
  189.6 3.4 %copy-start.5 = (f32[16,8,128]{2,1,0:T(8,128)S(1)}, f32[16,8,128]{2,1,0:T(8,128)}, u32[]{:S(2)}) copy-start(f32[16,8,128]{2,1,0:T(8,128)} %get-tuple-element.11) | copy-start | bytes 196612
  196.3 1.0 copy-start.20
  196.3 1.0 copy-start.23
  196.3 1.0 copy-start.26
where the time goes:
time: 200 us; the launch traced here: 199 us
  starting transfers between devices  134 us (67%)
  other arithmetic  37.5 us (19%)
  local copies, waits for them, and re-layouts  19 us (10%)
  waiting for transfers between devices  6.45 us (3%)
    ppermute x6, starting transfers between devices, with_halo(): lax.ppermute(lax.slice_in_dim(block, 0, width, axis=dim), axis, backward)  38.9 us
    ppermute x6, starting transfers between devices, padded_2(): lax.ppermute(leading, axis, [(b, a) for a, b in up])  34.1 us
    all_to_all x3, starting transfers between devices, body(): lax.all_to_all(velocity[2, -1], 'py', split_axis=1, concat_axis=0, tiled=...  18.1 us
    all_to_all x3, starting transfers between devices, body(): lax.all_to_all(air_field[0, 0], 'py', split_axis=1, concat_axis=0, tiled=...  17.7 us
    unnamed x18, other arithmetic  15.8 us
    ppermute x6, starting transfers between devices, with_halo(): lax.ppermute(lax.slice_in_dim(block, block.shape[dim] - width, None, axis...  13.1 us
    ppermute x6, starting transfers between devices, padded_2(): lax.ppermute(last, axis, up)  12 us
    all_to_all x3, waiting for transfers between devices, body(): lax.all_to_all(air_field[0, 0], 'py', split_axis=1, concat_axis=0, tiled=...  4.81 us
  transfers between devices with their start and end apart: 30, of which 3 were waited for; matrix products, arithmetic and copies ran while one was open for 21% of the time, Pallas kernels for 0%

commit v1 on v0

--- a/solution.py
+++ b/solution.py
@@ -232,7 +232,12 @@
         velocity = ground_velocity(
             velocity, strip_rim(stress), ground_buoyancy, pressure_plane, 1, 2
         )
-        surface = lax.all_to_all(velocity[2, -1], "py", split_axis=1, concat_axis=0, tiled=True).T
+        surface = jnp.concatenate(
+            lax.all_to_all(
+                jnp.stack(jnp.split(velocity[2, -1], lax.axis_size("py"), axis=1)), "py", 0, 0
+            ),
+            axis=0,
+        ).T
         air_field = air_update(
             air_field, air_bulk, air_buoyancy, air_wind, surface, west_inner, south_inner
         )

time: 200 us -> 232 us (1.16)
  local copies, waits for them, and re-layouts: 19 us -> 48.3 us
    unnamed x56 -> x101, local copies, waits for them, and re-layouts: 0.46 us -> 30 us
    all_to_all x9 -> x0, local copies, waits for them, and re-layouts: 3.55 us -> none  [body(): lax.all_to_all(velocity[2, -1], 'py', split_axis=1, concat_axis=0, tiled=...]
  transfers between devices with their start and end apart: 30 -> 30, of which waited for: 3 -> 3; matrix products, arithmetic and copies ran while one was open for 21% -> 31% of each run, Pallas kernels for 0% -> 0%
where the time goes in v1:
time: 232 us; the launch traced here: 230 us
  starting transfers between devices  136 us (59%)
  local copies, waits for them, and re-layouts  48.3 us (21%)
  other arithmetic  37.5 us (16%)
  waiting for transfers between devices  6.45 us (3%)
    ppermute x6, starting transfers between devices, with_halo(): lax.ppermute(lax.slice_in_dim(block, 0, width, axis=dim), axis, backward)  38.9 us
    ppermute x6, starting transfers between devices, padded_2(): lax.ppermute(leading, axis, [(b, a) for a, b in up])  34.1 us
    unnamed x101, local copies, waits for them, and re-layouts  30 us
    all_to_all x3, starting transfers between devices, body(): lax.all_to_all(jnp.stack(jnp.split(velocity[2, -1], lax.axis_size('py'),...  20.2 us
    all_to_all x3, starting transfers between devices, body(): lax.all_to_all(air_field[0, 0], 'py', split_axis=1, concat_axis=0, tiled=...  17.7 us
    unnamed x18, other arithmetic  15.8 us
    ppermute x6, starting transfers between devices, with_halo(): lax.ppermute(lax.slice_in_dim(block, block.shape[dim] - width, None, axis...  13.1 us
    ppermute x6, starting transfers between devices, padded_2(): lax.ppermute(last, axis, up)  11.9 us
  transfers between devices with their start and end apart: 30, of which 3 were waited for; matrix products, arithmetic and copies ran while one was open for 31% of the time, Pallas kernels for 0%

profile of v1, /device:TPU:96, one launch (start us, length us, event | category | flops | bytes accessed | tf_op | source)
XLA Modules:
  0.0 230.1 jit_solution(958619615206197724)
XLA Ops:
  2.1 5.9 %all-to-all-start = ((f32[8,16,8]{2,0,1:T(8,128)}), f32[8,16,8]{2,0,1:T(8,128)S(1)}, u32[]{:S(2)}, u32[]{:S(2)}) async-start(f32[8,16,8]{2,0,1:T(8,128)} %copy.21), calls=%async_computation | async-start | bytes 131072 | tf_op jit(solution)/shard_map/all_to_all | solution.py:229
  8.1 1.1 slice_select_fusion
  9.2 2.0 collective-permute-start.4
  11.3 5.6 %collective-permute-start.5 = (f32[6,16,1,128]{3,2,1,0:T(1,128)S(1)}, f32[6,16,1,128]{3,2,1,0:T(1,128)S(1)}, u32[]{:S(2)}, u32[]{:S(2)}) collective-permute-start(f32[6,16,1,128]{3,2,1,0:T(1,128)S(1)} %get-tuple-element.99), channel_id=1, source_target_pairs={{1,0},{2,1},{3,2},{4,3},{5,4},{6,5},{7,6},{8,7},{9,8},{10,9},{11,1... | collective-permute-start | bytes 147464 | tf_op jit(solution)/shard_map/ppermute | solution.py:31
  16.9 2.3 fusion.203
  19.2 3.4 %collective-permute-start = (f32[4,32,8,2]{3,2,1,0:T(8,128)}, f32[4,32,8,2]{3,2,1,0:T(8,128)S(1)}, u32[]{:S(2)}, u32[]{:S(2)}) collective-permute-start(f32[4,32,8,2]{3,2,1,0:T(8,128)} %get-tuple-element.92), channel_id=1, source_target_pairs={{0,16},{16,32},{32,48},{48,64},{64,80},{80,96},{96,112},{1,17},{17... | collective-permute-start | bytes 24584 | tf_op jit(solution)/shard_map/ppermute | solution.py:14
  22.6 6.1 %collective-permute-start.1 = (f32[4,32,8,2]{3,2,1,0:T(8,128)S(1)}, f32[4,32,8,2]{3,2,1,0:T(8,128)S(1)}, u32[]{:S(2)}, u32[]{:S(2)}) collective-permute-start(f32[4,32,8,2]{3,2,1,0:T(8,128)S(1)} %get-tuple-element.93), channel_id=1, source_target_pairs={{16,0},{32,16},{48,32},{64,48},{80,64},{96,80},{112,96},{17,1},{33... | collective-permute-start | bytes 24584 | tf_op jit(solution)/shard_map/ppermute | solution.py:17
  30.7 0.9 select_maximum_fusion.4
  32.4 1.0 fusion.173
  33.4 1.1 fusion.168
  34.6 1.9 collective-permute-start.10
  36.5 5.8 %collective-permute-start.11 = (f32[3,16,1,128]{3,2,1,0:T(1,128)S(1)}, f32[3,16,1,128]{3,2,1,0:T(1,128)S(1)}, u32[]{:S(2)}, u32[]{:S(2)}) collective-permute-start(f32[3,16,1,128]{3,2,1,0:T(1,128)S(1)} %get-tuple-element.119), channel_id=1, source_target_pairs={{1,0},{2,1},{3,2},{4,3},{5,4},{6,5},{7,6},{8,7},{9,8},{10,9},{11,1... | collective-permute-start | bytes 73736 | tf_op jit(solution)/shard_map/ppermute | solution.py:31
  52.8 7.6 %all-to-all-start.1 = ((f32[16,8,8]{2,1,0:T(8,128)}), f32[16,8,8]{2,1,0:T(8,128)S(1)}, u32[]{:S(2)}, u32[]{:S(2)}) async-start(f32[16,8,8]{2,1,0:T(8,128)} %constant_dynamic-update-slice_fusion), calls=%async_computation.1 | async-start | bytes 131072 | tf_op jit(solution)/shard_map/all_to_all | solution.py:236
  61.3 0.8 constant_dynamic-update-slice_fusion.21
  62.8 0.8 constant_dynamic-update-slice_fusion.19
  63.6 0.8 constant_dynamic-update-slice_fusion.18
  64.7 2.0 collective-permute-start.12
  66.8 5.6 %collective-permute-start.13 = (f32[6,16,1,128]{3,2,1,0:T(1,128)S(1)}, f32[6,16,1,128]{3,2,1,0:T(1,128)S(1)}, u32[]{:S(2)}, u32[]{:S(2)}) collective-permute-start(f32[6,16,1,128]{3,2,1,0:T(1,128)S(1)} %get-tuple-element.97), channel_id=1, source_target_pairs={{1,0},{2,1},{3,2},{4,3},{5,4},{6,5},{7,6},{8,7},{9,8},{10,9},{11,1... | collective-permute-start | bytes 147464 | tf_op jit(solution)/shard_map/ppermute | solution.py:31
  72.4 1.7 pad_maximum_fusion.20
  74.1 1.9 collective-permute-start.2
  76.0 5.8 %collective-permute-start.3 = (f32[4,32,2,132]{3,2,1,0:T(2,128)}, f32[4,32,2,132]{3,2,1,0:T(2,128)}, u32[]{:S(2)}, u32[]{:S(2)}) collective-permute-start(f32[4,32,2,132]{3,2,1,0:T(2,128)} %get-tuple-element.67), channel_id=1, source_target_pairs={{1,0},{2,1},{3,2},{4,3},{5,4},{6,5},{7,6},{8,7},{9,8},{10,9},{11,1... | collective-permute-start | bytes 405512 | tf_op jit(solution)/shard_map/ppermute | solution.py:17
  82.5 0.9 select_maximum_fusion.2
  84.7 1.3 collective-permute-done.3
  86.0 2.0 pad_maximum_fusion
  91.0 5.9 %all-to-all-start.2 = ((f32[8,16,8]{2,0,1:T(8,128)}), f32[8,16,8]{2,0,1:T(8,128)S(1)}, u32[]{:S(2)}, u32[]{:S(2)}) async-start(f32[8,16,8]{2,0,1:T(8,128)} %copy.24), calls=%async_computation.2 | async-start | bytes 131072 | tf_op jit(solution)/shard_map/all_to_all | solution.py:229
  96.9 4.8 %all-to-all-done.2 = f32[8,16,8]{2,0,1:T(8,128)S(1)} async-done(((f32[8,16,8]{2,0,1:T(8,128)}), f32[8,16,8]{2,0,1:T(8,128)S(1)}, u32[]{:S(2)}, u32[]{:S(2)}) %all-to-all-start.2) | async-done | bytes 4128 | tf_op jit(solution)/shard_map/all_to_all | solution.py:229
  102.0 2.0 collective-permute-start.18
  104.1 5.6 %collective-permute-start.19 = (f32[3,16,1,128]{3,2,1,0:T(1,128)S(1)}, f32[3,16,1,128]{3,2,1,0:T(1,128)S(1)}, u32[]{:S(2)}, u32[]{:S(2)}) collective-permute-start(f32[3,16,1,128]{3,2,1,0:T(1,128)S(1)} %get-tuple-element.117), channel_id=1, source_target_pairs={{1,0},{2,1},{3,2},{4,3},{5,4},{6,5},{7,6},{8,7},{9,8},{10,9},{11,1... | collective-permute-start | bytes 73736 | tf_op jit(solution)/shard_map/ppermute | solution.py:31
  120.3 6.8 %all-to-all-start.3 = ((f32[16,8,8]{2,1,0:T(8,128)}), f32[16,8,8]{2,1,0:T(8,128)S(1)}, u32[]{:S(2)}, u32[]{:S(2)}) async-start(f32[16,8,8]{2,1,0:T(8,128)} %constant_dynamic-update-slice_fusion.22), calls=%async_computation.3 | async-start | bytes 131072 | tf_op jit(solution)/shard_map/all_to_all | solution.py:236
  127.1 1.0 fusion.201
  128.1 1.9 collective-permute-start.6
  130.0 7.7 %collective-permute-start.7 = (f32[4,32,8,2]{3,2,1,0:T(8,128)S(1)}, f32[4,32,8,2]{3,2,1,0:T(8,128)S(1)}, u32[]{:S(2)}, u32[]{:S(2)}) collective-permute-start(f32[4,32,8,2]{3,2,1,0:T(8,128)S(1)} %get-tuple-element.88), channel_id=1, source_target_pairs={{16,0},{32,16},{48,32},{64,48},{80,64},{96,80},{112,96},{17,1},{33... | collective-permute-start | bytes 24584 | tf_op jit(solution)/shard_map/ppermute | solution.py:17
  139.2 1.6 constant_dynamic-update-slice_fusion.43
  140.8 1.6 constant_dynamic-update-slice_fusion.42
  142.4 0.8 constant_dynamic-update-slice_fusion.41
  143.2 0.8 constant_dynamic-update-slice_fusion.40
  144.9 1.9 collective-permute-start.20
  146.8 5.8 %collective-permute-start.21 = (f32[6,16,1,128]{3,2,1,0:T(1,128)S(1)}, f32[6,16,1,128]{3,2,1,0:T(1,128)S(1)}, u32[]{:S(2)}, u32[]{:S(2)}) collective-permute-start(f32[6,16,1,128]{3,2,1,0:T(1,128)S(1)} %get-tuple-element.95), channel_id=1, source_target_pairs={{1,0},{2,1},{3,2},{4,3},{5,4},{6,5},{7,6},{8,7},{9,8},{10,9},{11,1... | collective-permute-start | bytes 147464 | tf_op jit(solution)/shard_map/ppermute | solution.py:31
  152.6 0.9 pad_maximum_fusion.17
  153.5 1.9 collective-permute-start.8
  155.4 5.8 %collective-permute-start.9 = (f32[4,32,2,132]{3,2,1,0:T(2,128)S(1)}, f32[4,32,2,132]{3,2,1,0:T(2,128)S(1)}, u32[]{:S(2)}, u32[]{:S(2)}) collective-permute-start(f32[4,32,2,132]{3,2,1,0:T(2,128)S(1)} %get-tuple-element.65), channel_id=1, source_target_pairs={{1,0},{2,1},{3,2},{4,3},{5,4},{6,5},{7,6},{8,7},{9,8},{10,9},{11,1... | collective-permute-start | bytes 405512 | tf_op jit(solution)/shard_map/ppermute | solution.py:17
  161.2 0.9 select_maximum_fusion
  163.2 0.8 constant_dynamic-update-slice_fusion.68
  164.0 0.8 constant_dynamic-update-slice_fusion.67
  165.1 1.0 pad_maximum_fusion.1
  169.1 5.9 %all-to-all-start.4 = ((f32[8,16,8]{2,0,1:T(8,128)}), f32[8,16,8]{2,0,1:T(8,128)S(1)}, u32[]{:S(2)}, u32[]{:S(2)}) async-start(f32[8,16,8]{2,0,1:T(8,128)} %copy.27), calls=%async_computation.4 | async-start | bytes 131072 | tf_op jit(solution)/shard_map/all_to_all | solution.py:229
  175.0 1.1 fusion.199
  176.2 1.9 collective-permute-start.14
  178.1 7.5 %collective-permute-start.15 = (f32[4,32,8,2]{3,2,1,0:T(8,128)}, f32[4,32,8,2]{3,2,1,0:T(8,128)S(1)}, u32[]{:S(2)}, u32[]{:S(2)}) collective-permute-start(f32[4,32,8,2]{3,2,1,0:T(8,128)} %get-tuple-element.83), channel_id=1, source_target_pairs={{16,0},{32,16},{48,32},{64,48},{80,64},{96,80},{112,96},{17,1},{33... | collective-permute-start | bytes 24584 | tf_op jit(solution)/shard_map/ppermute | solution.py:17
  185.7 1.7 constant_dynamic-update-slice_fusion.66
  197.9 5.7 %all-to-all-start.5 = ((f32[16,8,8]{2,1,0:T(8,128)}), f32[16,8,8]{2,1,0:T(8,128)S(1)}, u32[]{:S(2)}, u32[]{:S(2)}) async-start(f32[16,8,8]{2,1,0:T(8,128)} %constant_dynamic-update-slice_fusion.44), calls=%async_computation.5 | async-start | bytes 131072 | tf_op jit(solution)/shard_map/all_to_all | solution.py:236
  203.7 2.0 collective-permute-start.22
  205.7 5.6 %collective-permute-start.23 = (f32[3,16,1,128]{3,2,1,0:T(1,128)S(1)}, f32[3,16,1,128]{3,2,1,0:T(1,128)S(1)}, u32[]{:S(2)}, u32[]{:S(2)}) collective-permute-start(f32[3,16,1,128]{3,2,1,0:T(1,128)S(1)} %get-tuple-element.115), channel_id=1, source_target_pairs={{1,0},{2,1},{3,2},{4,3},{5,4},{6,5},{7,6},{8,7},{9,8},{10,9},{11,1... | collective-permute-start | bytes 73736 | tf_op jit(solution)/shard_map/ppermute | solution.py:31
  211.4 0.9 pad_maximum_fusion.11
  212.3 2.1 collective-permute-start.16
  214.4 6.1 %collective-permute-start.17 = (f32[4,32,2,132]{3,2,1,0:T(2,128)S(1)}, f32[4,32,2,132]{3,2,1,0:T(2,128)S(1)}, u32[]{:S(2)}, u32[]{:S(2)}) collective-permute-start(f32[4,32,2,132]{3,2,1,0:T(2,128)S(1)} %get-tuple-element.57), channel_id=1, source_target_pairs={{1,0},{2,1},{3,2},{4,3},{5,4},{6,5},{7,6},{8,7},{9,8},{10,9},{11,1... | collective-permute-start | bytes 405512 | tf_op jit(solution)/shard_map/ppermute | solution.py:17
  221.4 0.8 constant_dynamic-update-slice_fusion.65
  222.2 0.8 constant_dynamic-update-slice_fusion.64
  222.9 0.8 constant_dynamic-update-slice_fusion.63
  223.7 0.8 constant_dynamic-update-slice_fusion.62
  224.5 0.8 constant_dynamic-update-slice_fusion.61
  225.2 0.8 constant_dynamic-update-slice_fusion.60
  226.0 1.0 pad_maximum_fusion.2
  229.3 0.8 pad_maximum_fusion.5
  (236 shorter events, 52.6 us)
Async XLA Ops:
  0.6 28.1 %copy-start.27 = (f32[2,32]{1,0:T(2,128)S(1)}, f32[2,32]{1,0:T(2,128)}, u32[]{:S(2)}) copy-start(f32[2,32]{1,0:T(2,128)} %param.10) | copy-start | bytes 772
  0.6 28.1 %copy-start.14 = (f32[32]{0:T(128)S(1)}, f32[32]{0:T(128)}, u32[]{:S(2)}) copy-start(f32[32]{0:T(128)} %param.9) | copy-start | bytes 388
  2.1 28.5 %all-to-all-start = ((f32[8,16,8]{2,0,1:T(8,128)}), f32[8,16,8]{2,0,1:T(8,128)S(1)}, u32[]{:S(2)}, u32[]{:S(2)}) async-start(f32[8,16,8]{2,0,1:T(8,128)} %copy.21), calls=%async_computation | async-start | bytes 131072 | tf_op jit(solution)/shard_map/all_to_all | solution.py:229
  9.2 21.4 %collective-permute-start.4 = (f32[6,16,1,128]{3,2,1,0:T(1,128)S(1)}, f32[6,16,1,128]{3,2,1,0:T(1,128)S(1)}, u32[]{:S(2)}, u32[]{:S(2)}) collective-permute-start(f32[6,16,1,128]{3,2,1,0:T(1,128)S(1)} %get-tuple-element.98), channel_id=1, source_target_pairs={{0,1},{1,2},{2,3},{3,4},{4,5},{5,6},{6,7},{7,8},{8,9},{9,10},{10,1... | collective-permute-start | bytes 147464 | tf_op jit(solution)/shard_map/ppermute | solution.py:30
  11.3 19.4 %collective-permute-start.5 = (f32[6,16,1,128]{3,2,1,0:T(1,128)S(1)}, f32[6,16,1,128]{3,2,1,0:T(1,128)S(1)}, u32[]{:S(2)}, u32[]{:S(2)}) collective-permute-start(f32[6,16,1,128]{3,2,1,0:T(1,128)S(1)} %get-tuple-element.99), channel_id=1, source_target_pairs={{1,0},{2,1},{3,2},{4,3},{5,4},{6,5},{7,6},{8,7},{9,8},{10,9},{11,1... | collective-permute-start | bytes 147464 | tf_op jit(solution)/shard_map/ppermute | solution.py:31
  19.2 53.2 %collective-permute-start = (f32[4,32,8,2]{3,2,1,0:T(8,128)}, f32[4,32,8,2]{3,2,1,0:T(8,128)S(1)}, u32[]{:S(2)}, u32[]{:S(2)}) collective-permute-start(f32[4,32,8,2]{3,2,1,0:T(8,128)} %get-tuple-element.92), channel_id=1, source_target_pairs={{0,16},{16,32},{32,48},{48,64},{64,80},{80,96},{96,112},{1,17},{17... | collective-permute-start | bytes 24584 | tf_op jit(solution)/shard_map/ppermute | solution.py:14
  22.6 49.8 %collective-permute-start.1 = (f32[4,32,8,2]{3,2,1,0:T(8,128)S(1)}, f32[4,32,8,2]{3,2,1,0:T(8,128)S(1)}, u32[]{:S(2)}, u32[]{:S(2)}) collective-permute-start(f32[4,32,8,2]{3,2,1,0:T(8,128)S(1)} %get-tuple-element.93), channel_id=1, source_target_pairs={{16,0},{32,16},{48,32},{64,48},{80,64},{96,80},{112,96},{17,1},{33... | collective-permute-start | bytes 24584 | tf_op jit(solution)/shard_map/ppermute | solution.py:17
  31.6 0.8 copy-start.2
  33.4 27.9 %copy-start = (f32[2,16,8,128]{3,2,1,0:T(8,128)S(1)}, f32[2,16,8,128]{3,2,1,0:T(8,128)}, u32[]{:S(2)}) copy-start(f32[2,16,8,128]{3,2,1,0:T(8,128)} %param.12) | copy-start | bytes 393220
  34.6 25.8 %collective-permute-start.10 = (f32[3,16,1,128]{3,2,1,0:T(1,128)S(1)}, f32[3,16,1,128]{3,2,1,0:T(1,128)S(1)}, u32[]{:S(2)}, u32[]{:S(2)}) collective-permute-start(f32[3,16,1,128]{3,2,1,0:T(1,128)S(1)} %get-tuple-element.118), channel_id=1, source_target_pairs={{0,1},{1,2},{2,3},{3,4},{4,5},{5,6},{6,7},{7,8},{8,9},{9,10},{10,1... | collective-permute-start | bytes 73736 | tf_op jit(solution)/shard_map/ppermute | solution.py:30
  36.5 23.9 %collective-permute-start.11 = (f32[3,16,1,128]{3,2,1,0:T(1,128)S(1)}, f32[3,16,1,128]{3,2,1,0:T(1,128)S(1)}, u32[]{:S(2)}, u32[]{:S(2)}) collective-permute-start(f32[3,16,1,128]{3,2,1,0:T(1,128)S(1)} %get-tuple-element.119), channel_id=1, source_target_pairs={{1,0},{2,1},{3,2},{4,3},{5,4},{6,5},{7,6},{8,7},{9,8},{10,9},{11,1... | collective-permute-start | bytes 73736 | tf_op jit(solution)/shard_map/ppermute | solution.py:31
  52.8 29.0 %all-to-all-start.1 = ((f32[16,8,8]{2,1,0:T(8,128)}), f32[16,8,8]{2,1,0:T(8,128)S(1)}, u32[]{:S(2)}, u32[]{:S(2)}) async-start(f32[16,8,8]{2,1,0:T(8,128)} %constant_dynamic-update-slice_fusion), calls=%async_computation.1 | async-start | bytes 131072 | tf_op jit(solution)/shard_map/all_to_all | solution.py:236
  60.9 3.4 %copy-start.15 = (pred[16]{0:T(512)(128)(4,1)S(1)}, pred[16]{0:T(512)(128)(4,1)}, u32[]{:S(2)}) copy-start(pred[16]{0:T(512)(128)(4,1)} %constant.29.clone.1) | copy-start | bytes 52
  61.1 11.3 %copy-start.1 = (f32[4,32,8,128]{3,2,1,0:T(8,128)S(1)}, f32[4,32,8,128]{3,2,1,0:T(8,128)}, u32[]{:S(2)}) copy-start(f32[4,32,8,128]{3,2,1,0:T(8,128)} %param.7) | copy-start | bytes 1572868
  64.7 17.7 %collective-permute-start.12 = (f32[6,16,1,128]{3,2,1,0:T(1,128)S(1)}, f32[6,16,1,128]{3,2,1,0:T(1,128)S(1)}, u32[]{:S(2)}, u32[]{:S(2)}) collective-permute-start(f32[6,16,1,128]{3,2,1,0:T(1,128)S(1)} %get-tuple-element.96), channel_id=1, source_target_pairs={{0,1},{1,2},{2,3},{3,4},{4,5},{5,6},{6,7},{7,8},{8,9},{9,10},{10,1... | collective-permute-start | bytes 147464 | tf_op jit(solution)/shard_map/ppermute | solution.py:30
  66.8 15.7 %collective-permute-start.13 = (f32[6,16,1,128]{3,2,1,0:T(1,128)S(1)}, f32[6,16,1,128]{3,2,1,0:T(1,128)S(1)}, u32[]{:S(2)}, u32[]{:S(2)}) collective-permute-start(f32[6,16,1,128]{3,2,1,0:T(1,128)S(1)} %get-tuple-element.97), channel_id=1, source_target_pairs={{1,0},{2,1},{3,2},{4,3},{5,4},{6,5},{7,6},{8,7},{9,8},{10,9},{11,1... | collective-permute-start | bytes 147464 | tf_op jit(solution)/shard_map/ppermute | solution.py:31
  74.1 10.6 %collective-permute-start.2 = (f32[4,32,2,132]{3,2,1,0:T(2,128)}, f32[4,32,2,132]{3,2,1,0:T(2,128)}, u32[]{:S(2)}, u32[]{:S(2)}) collective-permute-start(f32[4,32,2,132]{3,2,1,0:T(2,128)} %get-tuple-element.66), channel_id=1, source_target_pairs={{0,1},{1,2},{2,3},{3,4},{4,5},{5,6},{6,7},{7,8},{8,9},{9,10},{10,1... | collective-permute-start | bytes 405512 | tf_op jit(solution)/shard_map/ppermute | solution.py:14
  76.0 9.9 %collective-permute-start.3 = (f32[4,32,2,132]{3,2,1,0:T(2,128)}, f32[4,32,2,132]{3,2,1,0:T(2,128)}, u32[]{:S(2)}, u32[]{:S(2)}) collective-permute-start(f32[4,32,2,132]{3,2,1,0:T(2,128)} %get-tuple-element.67), channel_id=1, source_target_pairs={{1,0},{2,1},{3,2},{4,3},{5,4},{6,5},{7,6},{8,7},{9,8},{10,9},{11,1... | collective-permute-start | bytes 405512 | tf_op jit(solution)/shard_map/ppermute | solution.py:17
  88.9 0.9 copy-start.18
  88.9 0.9 copy-start.21
  88.9 0.9 copy-start.24
  88.9 1.1 copy-start.3
  88.9 1.1 copy-start.17
  89.6 12.2 %copy-start.13 = (f32[15,8,128]{2,1,0:T(8,128)S(1)}, f32[15,8,128]{2,1,0:T(8,128)}, u32[]{:S(2)}) copy-start(f32[15,8,128]{2,1,0:T(8,128)} %slice.1109) | copy-start | bytes 184324
  91.0 10.7 %all-to-all-start.2 = ((f32[8,16,8]{2,0,1:T(8,128)}), f32[8,16,8]{2,0,1:T(8,128)S(1)}, u32[]{:S(2)}, u32[]{:S(2)}) async-start(f32[8,16,8]{2,0,1:T(8,128)} %copy.24), calls=%async_computation.2 | async-start | bytes 131072 | tf_op jit(solution)/shard_map/all_to_all | solution.py:229
  102.0 36.4 %collective-permute-start.18 = (f32[3,16,1,128]{3,2,1,0:T(1,128)S(1)}, f32[3,16,1,128]{3,2,1,0:T(1,128)S(1)}, u32[]{:S(2)}, u32[]{:S(2)}) collective-permute-start(f32[3,16,1,128]{3,2,1,0:T(1,128)S(1)} %get-tuple-element.116), channel_id=1, source_target_pairs={{0,1},{1,2},{2,3},{3,4},{4,5},{5,6},{6,7},{7,8},{8,9},{9,10},{10,1... | collective-permute-start | bytes 73736 | tf_op jit(solution)/shard_map/ppermute | solution.py:30
  104.1 34.3 %collective-permute-start.19 = (f32[3,16,1,128]{3,2,1,0:T(1,128)S(1)}, f32[3,16,1,128]{3,2,1,0:T(1,128)S(1)}, u32[]{:S(2)}, u32[]{:S(2)}) collective-permute-start(f32[3,16,1,128]{3,2,1,0:T(1,128)S(1)} %get-tuple-element.117), channel_id=1, source_target_pairs={{1,0},{2,1},{3,2},{4,3},{5,4},{6,5},{7,6},{8,7},{9,8},{10,9},{11,1... | collective-permute-start | bytes 73736 | tf_op jit(solution)/shard_map/ppermute | solution.py:31
  120.3 17.5 %all-to-all-start.3 = ((f32[16,8,8]{2,1,0:T(8,128)}), f32[16,8,8]{2,1,0:T(8,128)S(1)}, u32[]{:S(2)}, u32[]{:S(2)}) async-start(f32[16,8,8]{2,1,0:T(8,128)} %constant_dynamic-update-slice_fusion.22), calls=%async_computation.3 | async-start | bytes 131072 | tf_op jit(solution)/shard_map/all_to_all | solution.py:236
  128.1 24.5 %collective-permute-start.6 = (f32[4,32,8,2]{3,2,1,0:T(8,128)}, f32[4,32,8,2]{3,2,1,0:T(8,128)S(1)}, u32[]{:S(2)}, u32[]{:S(2)}) collective-permute-start(f32[4,32,8,2]{3,2,1,0:T(8,128)} %get-tuple-element.87), channel_id=1, source_target_pairs={{0,16},{16,32},{32,48},{48,64},{64,80},{80,96},{96,112},{1,17},{17... | collective-permute-start | bytes 24584 | tf_op jit(solution)/shard_map/ppermute | solution.py:14
  130.0 22.6 %collective-permute-start.7 = (f32[4,32,8,2]{3,2,1,0:T(8,128)S(1)}, f32[4,32,8,2]{3,2,1,0:T(8,128)S(1)}, u32[]{:S(2)}, u32[]{:S(2)}) collective-permute-start(f32[4,32,8,2]{3,2,1,0:T(8,128)S(1)} %get-tuple-element.88), channel_id=1, source_target_pairs={{16,0},{32,16},{48,32},{64,48},{80,64},{96,80},{112,96},{17,1},{33... | collective-permute-start | bytes 24584 | tf_op jit(solution)/shard_map/ppermute | solution.py:17
  138.4 4.0 %copy-start.11 = (f32[16,8,128]{2,1,0:T(8,128)S(1)}, f32[16,8,128]{2,1,0:T(8,128)}, u32[]{:S(2)}) copy-start(f32[16,8,128]{2,1,0:T(8,128)} %get-tuple-element.27) | copy-start | bytes 196612
  138.9 4.3 %copy-start.10 = (f32[16,8,128]{2,1,0:T(8,128)S(1)}, f32[16,8,128]{2,1,0:T(8,128)}, u32[]{:S(2)}) copy-start(f32[16,8,128]{2,1,0:T(8,128)} %get-tuple-element.25) | copy-start | bytes 196612
  144.9 16.3 %collective-permute-start.20 = (f32[6,16,1,128]{3,2,1,0:T(1,128)S(1)}, f32[6,16,1,128]{3,2,1,0:T(1,128)S(1)}, u32[]{:S(2)}, u32[]{:S(2)}) collective-permute-start(f32[6,16,1,128]{3,2,1,0:T(1,128)S(1)} %get-tuple-element.94), channel_id=1, source_target_pairs={{0,1},{1,2},{2,3},{3,4},{4,5},{5,6},{6,7},{7,8},{8,9},{9,10},{10,1... | collective-permute-start | bytes 147464 | tf_op jit(solution)/shard_map/ppermute | solution.py:30
  146.8 14.4 %collective-permute-start.21 = (f32[6,16,1,128]{3,2,1,0:T(1,128)S(1)}, f32[6,16,1,128]{3,2,1,0:T(1,128)S(1)}, u32[]{:S(2)}, u32[]{:S(2)}) collective-permute-start(f32[6,16,1,128]{3,2,1,0:T(1,128)S(1)} %get-tuple-element.95), channel_id=1, source_target_pairs={{1,0},{2,1},{3,2},{4,3},{5,4},{6,5},{7,6},{8,7},{9,8},{10,9},{11,1... | collective-permute-start | bytes 147464 | tf_op jit(solution)/shard_map/ppermute | solution.py:31
  153.5 11.3 %collective-permute-start.8 = (f32[4,32,2,132]{3,2,1,0:T(2,128)S(1)}, f32[4,32,2,132]{3,2,1,0:T(2,128)S(1)}, u32[]{:S(2)}, u32[]{:S(2)}) collective-permute-start(f32[4,32,2,132]{3,2,1,0:T(2,128)S(1)} %get-tuple-element.64), channel_id=1, source_target_pairs={{0,1},{1,2},{2,3},{3,4},{4,5},{5,6},{6,7},{7,8},{8,9},{9,10},{10,1... | collective-permute-start | bytes 405512 | tf_op jit(solution)/shard_map/ppermute | solution.py:14
  155.4 9.6 %collective-permute-start.9 = (f32[4,32,2,132]{3,2,1,0:T(2,128)S(1)}, f32[4,32,2,132]{3,2,1,0:T(2,128)S(1)}, u32[]{:S(2)}, u32[]{:S(2)}) collective-permute-start(f32[4,32,2,132]{3,2,1,0:T(2,128)S(1)} %get-tuple-element.65), channel_id=1, source_target_pairs={{1,0},{2,1},{3,2},{4,3},{5,4},{6,5},{7,6},{8,7},{9,8},{10,9},{11,1... | collective-permute-start | bytes 405512 | tf_op jit(solution)/shard_map/ppermute | solution.py:17
  162.3 2.5 %copy-start.4 = (f32[16,10,130]{2,1,0:T(8,128)}, f32[16,10,130]{2,1,0:T(8,128)S(1)}, u32[]{:S(2)}) copy-start(f32[16,10,130]{2,1,0:T(8,128)S(1)} %get-tuple-element.44) | copy-start | bytes 249604
  166.8 1.0 copy-start.19
  166.9 1.0 copy-start.22
  166.9 1.0 copy-start.25
  166.9 1.2 copy-start.16
  168.4 17.3 %copy-start.12 = (f32[15,8,128]{2,1,0:T(8,128)S(1)}, f32[15,8,128]{2,1,0:T(8,128)}, u32[]{:S(2)}) copy-start(f32[15,8,128]{2,1,0:T(8,128)} %slice.1183) | copy-start | bytes 184324
  169.1 16.5 %all-to-all-start.4 = ((f32[8,16,8]{2,0,1:T(8,128)}), f32[8,16,8]{2,0,1:T(8,128)S(1)}, u32[]{:S(2)}, u32[]{:S(2)}) async-start(f32[8,16,8]{2,0,1:T(8,128)} %copy.27), calls=%async_computation.4 | async-start | bytes 131072 | tf_op jit(solution)/shard_map/all_to_all | solution.py:229
  176.2 35.3 %collective-permute-start.14 = (f32[4,32,8,2]{3,2,1,0:T(8,128)}, f32[4,32,8,2]{3,2,1,0:T(8,128)S(1)}, u32[]{:S(2)}, u32[]{:S(2)}) collective-permute-start(f32[4,32,8,2]{3,2,1,0:T(8,128)} %get-tuple-element.82), channel_id=1, source_target_pairs={{0,16},{16,32},{32,48},{48,64},{64,80},{80,96},{96,112},{1,17},{17... | collective-permute-start | bytes 24584 | tf_op jit(solution)/shard_map/ppermute | solution.py:14
  178.1 33.3 %collective-permute-start.15 = (f32[4,32,8,2]{3,2,1,0:T(8,128)}, f32[4,32,8,2]{3,2,1,0:T(8,128)S(1)}, u32[]{:S(2)}, u32[]{:S(2)}) collective-permute-start(f32[4,32,8,2]{3,2,1,0:T(8,128)} %get-tuple-element.83), channel_id=1, source_target_pairs={{16,0},{32,16},{48,32},{64,48},{80,64},{96,80},{112,96},{17,1},{33... | collective-permute-start | bytes 24584 | tf_op jit(solution)/shard_map/ppermute | solution.py:17
  197.9 13.4 %all-to-all-start.5 = ((f32[16,8,8]{2,1,0:T(8,128)}), f32[16,8,8]{2,1,0:T(8,128)S(1)}, u32[]{:S(2)}, u32[]{:S(2)}) async-start(f32[16,8,8]{2,1,0:T(8,128)} %constant_dynamic-update-slice_fusion.44), calls=%async_computation.5 | async-start | bytes 131072 | tf_op jit(solution)/shard_map/all_to_all | solution.py:236
  203.7 16.9 %collective-permute-start.22 = (f32[3,16,1,128]{3,2,1,0:T(1,128)S(1)}, f32[3,16,1,128]{3,2,1,0:T(1,128)S(1)}, u32[]{:S(2)}, u32[]{:S(2)}) collective-permute-start(f32[3,16,1,128]{3,2,1,0:T(1,128)S(1)} %get-tuple-element.114), channel_id=1, source_target_pairs={{0,1},{1,2},{2,3},{3,4},{4,5},{5,6},{6,7},{7,8},{8,9},{9,10},{10,1... | collective-permute-start | bytes 73736 | tf_op jit(solution)/shard_map/ppermute | solution.py:30
  205.7 14.8 %collective-permute-start.23 = (f32[3,16,1,128]{3,2,1,0:T(1,128)S(1)}, f32[3,16,1,128]{3,2,1,0:T(1,128)S(1)}, u32[]{:S(2)}, u32[]{:S(2)}) collective-permute-start(f32[3,16,1,128]{3,2,1,0:T(1,128)S(1)} %get-tuple-element.115), channel_id=1, source_target_pairs={{1,0},{2,1},{3,2},{4,3},{5,4},{6,5},{7,6},{8,7},{9,8},{10,9},{11,1... | collective-permute-start | bytes 73736 | tf_op jit(solution)/shard_map/ppermute | solution.py:31
  211.4 10.0 %copy-start.6 = (f32[16,8,128]{2,1,0:T(8,128)S(1)}, f32[16,8,128]{2,1,0:T(8,128)}, u32[]{:S(2)}) copy-start(f32[16,8,128]{2,1,0:T(8,128)} %get-tuple-element.19) | copy-start | bytes 196612
  212.3 9.8 %copy-start.7 = (f32[16,8,128]{2,1,0:T(8,128)S(1)}, f32[16,8,128]{2,1,0:T(8,128)}, u32[]{:S(2)}) copy-start(f32[16,8,128]{2,1,0:T(8,128)} %get-tuple-element.17) | copy-start | bytes 196612
  212.3 13.7 %collective-permute-start.16 = (f32[4,32,2,132]{3,2,1,0:T(2,128)S(1)}, f32[4,32,2,132]{3,2,1,0:T(2,128)S(1)}, u32[]{:S(2)}, u32[]{:S(2)}) collective-permute-start(f32[4,32,2,132]{3,2,1,0:T(2,128)S(1)} %get-tuple-element.56), channel_id=1, source_target_pairs={{0,1},{1,2},{2,3},{3,4},{4,5},{5,6},{6,7},{7,8},{8,9},{9,10},{10,1... | collective-permute-start | bytes 405512 | tf_op jit(solution)/shard_map/ppermute | solution.py:14
  214.4 8.5 %copy-start.8 = (f32[16,8,128]{2,1,0:T(8,128)S(1)}, f32[16,8,128]{2,1,0:T(8,128)}, u32[]{:S(2)}) copy-start(f32[16,8,128]{2,1,0:T(8,128)} %get-tuple-element.15) | copy-start | bytes 196612
  214.4 11.6 %collective-permute-start.17 = (f32[4,32,2,132]{3,2,1,0:T(2,128)S(1)}, f32[4,32,2,132]{3,2,1,0:T(2,128)S(1)}, u32[]{:S(2)}, u32[]{:S(2)}) collective-permute-start(f32[4,32,2,132]{3,2,1,0:T(2,128)S(1)} %get-tuple-element.57), channel_id=1, source_target_pairs={{1,0},{2,1},{3,2},{4,3},{5,4},{6,5},{7,6},{8,7},{9,8},{10,9},{11,1... | collective-permute-start | bytes 405512 | tf_op jit(solution)/shard_map/ppermute | solution.py:17
  221.0 2.7 %copy-start.9 = (f32[16,8,128]{2,1,0:T(8,128)S(1)}, f32[16,8,128]{2,1,0:T(8,128)}, u32[]{:S(2)}) copy-start(f32[16,8,128]{2,1,0:T(8,128)} %get-tuple-element.13) | copy-start | bytes 196612
  221.0 3.4 %copy-start.5 = (f32[16,8,128]{2,1,0:T(8,128)S(1)}, f32[16,8,128]{2,1,0:T(8,128)}, u32[]{:S(2)}) copy-start(f32[16,8,128]{2,1,0:T(8,128)} %get-tuple-element.11) | copy-start | bytes 196612
  227.7 1.0 copy-start.20
  227.7 1.0 copy-start.23
  227.8 1.0 copy-start.26
